TPU v7x, 32 devices: a whole 2x2x4 slice. The times are simulated.
32 devices in a mesh: dp: 8 (over z, x), tensor: 4 (over y, core).
Axes of the slice: x: 2, y: 2, z: 4, core: 2. Of those that a mesh axis runs over, the one named last changes fastest.
Arguments:
- tokens: bfloat16 [8192, 1024], P('dp'), may hold values from -6 to 6
- cotangent: bfloat16 [8192, 1024], P('dp'), may hold values from -6 to 6
- segments: int32 [8, 1024], P('dp'), may hold values from 0 to 3, never falling along the last dimension, each value on 1 to 512 neighbouring positions
- norm_gain: float32 [1024], replicated, may hold values from 0.5 to 1.5
- gate_proj: bfloat16 [1024, 2048], P(None, 'tensor'), may hold values from -0.1875 to 0.1875
- value_proj: bfloat16 [1024, 2048], P(None, 'tensor'), may hold values from -0.1875 to 0.1875
- shared_proj: bfloat16 [1024, 256], replicated, may hold values from -0.1875 to 0.1875
- step_proj: bfloat16 [1024, 32], P(None, 'tensor'), may hold values from -0.1875 to 0.1875
- conv_value: float32 [4, 2048], P(None, 'tensor'), may hold values from -3 to 3
- bias_value: float32 [2048], P('tensor'), may hold values from -3 to 3
- conv_shared: float32 [4, 256], replicated, may hold values from -3 to 3
- bias_shared: float32 [256], replicated, may hold values from -3 to 3
- step_bias: float32 [32], P('tensor'), may hold values from -3 to -1
- decay_log: float32 [32], P('tensor'), may hold values from -4 to 0.5
- skip_gain: float32 [32], P('tensor'), may hold values from 0.5 to 1.5
- gate_gain: float32 [2048], P('tensor'), may hold values from 0.5 to 1.5
- out_proj: bfloat16 [1024, 2048], P(None, 'tensor'), may hold values from -0.125 to 0.125
Outputs:
- result: bfloat16 [8192, 1024], P('dp')
- grad_tokens: bfloat16 [8192, 1024], P('dp')
- grad_norm_gain: float32 [1024], P('tensor')
- grad_gate_proj: float32 [1024, 2048], P('dp', 'tensor')
- grad_value_proj: float32 [1024, 2048], P('dp', 'tensor')
- grad_shared_proj: float32 [1024, 256], P('dp')
- grad_step_proj: float32 [1024, 32], P('dp', 'tensor')
- grad_conv_value: float32 [4, 2048], P(None, 'tensor')
- grad_bias_value: float32 [2048], P('tensor')
- grad_conv_shared: float32 [4, 256], replicated
- grad_bias_shared: float32 [256], replicated
- grad_step_bias: float32 [32], P('tensor')
- grad_decay_log: float32 [32], P('tensor')
- grad_skip_gain: float32 [32], P('tensor')
- grad_gate_gain: float32 [2048], P('tensor')
- grad_out_proj: float32 [1024, 2048], P('dp', 'tensor')
Inputs may be any that keep to these rules, and one draw needn't show every extreme that they name: `segments`: within a row of 1024 tokens the numbers never fall; a segment holds 1 to 512 tokens.
All inputs are finite; a program needn't handle non-finite values.
Results may differ from a plain program's by a relative error of at most 0.012.
Values may be sent and summed in bfloat16 or wider, within the bound.
A program may use at most 192 MiB of HBM per device.

v0:
```python
import jax
import jax.numpy as jnp
from jax import lax
from jax.experimental import pallas as pl
from jax.experimental.pallas import tpu as pltpu
from jax.sharding import PartitionSpec as P

SPAN = 256
HSIZE = 64
LANES = 128
EPSILON = 1e-05
NEG_FILL = -1e30
EXACT = lax.Precision.HIGHEST
F32 = jnp.float32
BF16 = jnp.bfloat16


def mm(left, right):
    return jnp.dot(left, right, preferred_element_type=F32)


def mm_t(left, right):
    return lax.dot_general(left, right, (((1,), (1,)), ((), ())), preferred_element_type=F32)


def t_mm(left, right):
    return lax.dot_general(left, right, (((0,), (0,)), ((), ())), preferred_element_type=F32)


def exact(left, right):
    return jnp.dot(left, right, precision=EXACT, preferred_element_type=F32)


def sigmoid(v):
    return 1.0 / (1.0 + jnp.exp(-v))


def spread(cols, pairs):
    low = lax.broadcasted_iota(jnp.int32, (cols.shape[0], LANES), 1) < HSIZE
    parts = [
        jnp.where(low, cols[:, 2 * p : 2 * p + 1], cols[:, 2 * p + 1 : 2 * p + 2])
        for p in range(pairs)
    ]
    return jnp.concatenate(parts, axis=1)


def gather_mat(inner):
    channel = lax.broadcasted_iota(jnp.int32, (inner, LANES), 0) // HSIZE
    head = lax.broadcasted_iota(jnp.int32, (inner, LANES), 1)
    return (channel == head).astype(F32)


def grid_masks():
    row = lax.broadcasted_iota(jnp.int32, (SPAN, SPAN), 0)
    col = lax.broadcasted_iota(jnp.int32, (SPAN, SPAN), 1)
    return row, col


def conv_fwd(buf, pack, aux):
    out = pack[4:5, :] + buf[8 : 8 + SPAN, :] * pack[3:4, :]
    for j in range(1, 4):
        out = out + buf[8 - j : 8 - j + SPAN, :] * (aux[:, j : j + 1] * pack[3 - j : 4 - j, :])
    return out


def fwd_kernel(
    tok, cot, aux_ref, segr, ng, wg, wv, ws, wst, wo, chp, shp, hp,
    hidden_o, gate_o, vpre_o, cv_o, spre_o, scv_o, z_o, ld_o, ldt_o, yn_o, sin_o, gn_o, stat_o,
    vbuf, sbuf, state,
):
    inner = wg.shape[1]
    pairs = inner // LANES
    state_size = ws.shape[1] // 2

    @pl.when(pl.program_id(0) == 0)
    def _():
        vbuf[0:8, :] = jnp.zeros((8, inner), F32)
        sbuf[0:8, :] = jnp.zeros((8, 2 * state_size), F32)
        state[...] = jnp.zeros_like(state)

    aux = aux_ref[...]
    x = tok[...].astype(F32)
    inv = lax.rsqrt(jnp.mean(x * x, axis=1, keepdims=True) + EPSILON)
    hid = (x * inv * ng[...]).astype(BF16)
    hidden_o[...] = hid
    gate = mm(hid, wg[...])
    gate_o[...] = gate
    vp = mm(hid, wv[...])
    vpre_o[...] = vp
    vbuf[8 : 8 + SPAN, :] = vp
    sp = mm(hid, ws[...])
    spre_o[...] = sp
    sbuf[8 : 8 + SPAN, :] = sp
    z = mm(hid, wst[...]) + hp[0:1, :]
    z_o[...] = z
    gn = mm(cot[...], wo[...])
    gn_o[...] = gn
    scv = conv_fwd(sbuf, shp, aux)
    scv_o[...] = scv
    bc = (scv * sigmoid(scv)).astype(BF16)
    b_low, c_low = bc[:, :state_size], bc[:, state_size:]
    cv = conv_fwd(vbuf, chp, aux)
    cv_o[...] = cv
    vbuf[0:8, :] = vbuf[SPAN : SPAN + 8, :]
    sbuf[0:8, :] = sbuf[SPAN : SPAN + 8, :]
    values = cv * sigmoid(cv)
    dt = jnp.maximum(z, 0.0) + jnp.log1p(jnp.exp(-jnp.abs(z)))
    row, col = grid_masks()
    tri = (row >= col).astype(F32)
    ld = exact(tri, dt * hp[1:2, :])
    ld_o[...] = ld
    ldt = jnp.transpose(ld)[0:8, :]
    ldt_o[...] = ldt
    allowed = (row >= col) & (aux[:, 0:1] == segr[...])
    scores = jnp.where(allowed, mm_t(c_low, b_low), 0.0)
    xs = values * spread(dt, pairs)
    xs_low = xs.astype(BF16)
    ein = jnp.exp(ld) * aux[:, 4:5]
    eout = jnp.exp(ld[SPAN - 1 : SPAN, :] - ld) * aux[:, 5:6]
    ein_x = spread(ein, pairs)
    eout_x = spread(eout, pairs)
    old = state[...]
    sin_o[...] = old
    carried = mm(c_low, old.astype(BF16)) * ein_x
    state[...] = old * ein_x[SPAN - 1 : SPAN, :] + t_mm(b_low, (xs * eout_x).astype(BF16))
    low = lax.broadcasted_iota(jnp.int32, (SPAN, LANES), 1) < HSIZE
    parts = []
    for p in range(pairs):
        pair = xs_low[:, p * LANES : (p + 1) * LANES]
        outs = []
        for h in (2 * p, 2 * p + 1):
            gap = jnp.minimum(ld[:, h : h + 1] - ldt[h : h + 1, :], 0.0)
            outs.append(mm((jnp.exp(gap) * scores).astype(BF16), pair))
        parts.append(jnp.where(low, outs[0], outs[1]))
    yn = jnp.concatenate(parts, axis=1) + carried
    yn_o[...] = yn
    gated = (yn + chp[6:7, :] * values) * (gate * sigmoid(gate))
    squares = jnp.sum(gated * gated, axis=1, keepdims=True)
    dots = jnp.sum(gn * chp[5:6, :] * gated, axis=1, keepdims=True)
    lane = lax.broadcasted_iota(jnp.int32, (SPAN, LANES), 1)
    both = jnp.where(lane == 0, squares, jnp.where(lane == 1, dots, 0.0))
    stat_o[...] = jnp.transpose(both)[0:8, :]


def gate_kernel(
    width, gate_ref, cv_ref, yn, gn_ref, stat, chp, wo, normal_o, dy_o, low_o, gain_o, mixed_o
):
    both = jnp.transpose(jnp.concatenate([stat[...]] * (LANES // 8), axis=0))
    inv = lax.rsqrt(both[:, 0:1] / width + EPSILON)
    mean_dots = both[:, 1:2] / width
    gate = gate_ref[...]
    cv = cv_ref[...]
    gn = gn_ref[...]
    sig = sigmoid(gate)
    act = gate * sig
    mixer = yn[...] + chp[6:7, :] * (cv * sigmoid(cv))
    gated = mixer * act
    normed = gated * inv
    normal = (normed * chp[5:6, :]).astype(BF16)
    normal_o[...] = normal
    mixed_o[...] = mm_t(normal, wo[...]).astype(BF16)
    part = jnp.sum(gn * normed, axis=0, keepdims=True)

    @pl.when(pl.program_id(0) == 0)
    def _():
        gain_o[...] = jnp.zeros_like(gain_o)

    gain_o[0:1, :] += part
    grad_gated = inv * (gn * chp[5:6, :]) - gated * (inv * inv * inv) * mean_dots
    dy_o[...] = grad_gated * act
    low_o[...] = (grad_gated * mixer * (sig * (1.0 + gate * (1.0 - sig)))).astype(BF16)


def bwd_kernel(
    dy_ref, cv_ref, vpre, scv_ref, z_ref, ld_ref, ldt_ref, yn, sin, aux_ref, segr, glow,
    wg, wv, wst, chp, hp,
    vlow_o, slow_o, dbc_o, heads_o, chg_o, hg_o,
    dbuf, dstate,
):
    inner = wg.shape[1]
    pairs = inner // LANES
    state_size = sin.shape[0]

    @pl.when(pl.program_id(0) == 0)
    def _():
        dbuf[SPAN : SPAN + 8, :] = jnp.zeros((8, inner), F32)
        dstate[...] = jnp.zeros_like(dstate)
        chg_o[...] = jnp.zeros_like(chg_o)
        hg_o[...] = jnp.zeros_like(hg_o)

    aux = aux_ref[...]
    dy = dy_ref[...]
    dy_low = dy.astype(BF16)
    scv = scv_ref[...]
    bc = (scv * sigmoid(scv)).astype(BF16)
    b_low, c_low = bc[:, :state_size], bc[:, state_size:]
    cv = cv_ref[...]
    csig = sigmoid(cv)
    values = cv * csig
    z = z_ref[...]
    dt = jnp.maximum(z, 0.0) + jnp.log1p(jnp.exp(-jnp.abs(z)))
    ld = ld_ref[...]
    ldt = ldt_ref[...]
    dt_x = spread(dt, pairs)
    xs = values * dt_x
    xs_low = xs.astype(BF16)
    ein = jnp.exp(ld) * aux[:, 4:5]
    eout = jnp.exp(ld[SPAN - 1 : SPAN, :] - ld) * aux[:, 5:6]
    ein_x = spread(ein, pairs)
    eout_x = spread(eout, pairs)
    row, col = grid_masks()
    allowed = (col >= row) & (aux[:, 0:1] == segr[...])
    mask = allowed.astype(F32)
    scores_t = mm_t(b_low, c_low) * mask
    low = lax.broadcasted_iota(jnp.int32, (SPAN, LANES), 1) < HSIZE
    parts = []
    dscores_t = jnp.zeros((SPAN, SPAN), F32)
    for p in range(pairs):
        cols = slice(p * LANES, (p + 1) * LANES)
        dy_pair = dy_low[:, cols]
        xs_pair = xs_low[:, cols]
        zero = jnp.zeros_like(xs_pair)
        outs = []
        for side, h in enumerate((2 * p, 2 * p + 1)):
            gap = jnp.minimum(ldt[h : h + 1, :] - ld[:, h : h + 1], 0.0)
            decay = jnp.exp(gap)
            outs.append(mm((decay * scores_t).astype(BF16), dy_pair))
            mine = jnp.where(low, xs_pair, zero) if side == 0 else jnp.where(low, zero, xs_pair)
            dscores_t = dscores_t + mm_t(mine, dy_pair) * decay
        parts.append(jnp.where(low, outs[0], outs[1]))
    inside = jnp.concatenate(parts, axis=1)
    dscores_low = (dscores_t * mask).astype(BF16)
    old = sin[...]
    dst = dstate[...]
    dst_low = dst.astype(BF16)
    dye_low = (dy * ein_x).astype(BF16)
    xse_low = (xs * eout_x).astype(BF16)
    db = mm(dscores_low, c_low) + mm_t(xse_low, dst_low)
    dc = t_mm(dscores_low, b_low) + mm_t(dye_low, old.astype(BF16))
    dbc_o[...] = jnp.concatenate([db, dc], axis=1)
    late = mm(b_low, dst_low) * eout_x
    keep = ein_x[SPAN - 1 : SPAN, :]
    dstate[...] = dst * keep + t_mm(c_low, dye_low)
    dxs = inside + late
    collect = gather_mat(inner)
    q = dy_low.astype(F32) * yn[...] - xs_low.astype(F32) * inside
    u = xs * late
    kappa = exact(jnp.sum(old * dst, axis=0, keepdims=True) * keep + jnp.zeros((8, inner), F32), collect)
    da = (
        exact((col >= row).astype(F32), exact(q, collect))
        + exact((row > col).astype(F32), exact(u, collect))
        + kappa[0:1, :]
    )
    rates = hp[1:2, :]
    ddt = da * rates + exact(dxs * values, collect)
    dz = ddt * sigmoid(z)
    slow = dz.astype(BF16)
    slow_o[...] = slow
    skip = exact(jnp.sum(dy * values, axis=0, keepdims=True) + jnp.zeros((8, inner), F32), collect)
    hg_o[0:1, :] += jnp.sum(dz, axis=0, keepdims=True)
    hg_o[1:2, :] += jnp.sum(da * dt, axis=0, keepdims=True) * rates
    hg_o[2:3, :] += skip[0:1, :]
    dcv = (dxs * dt_x + chp[6:7, :] * dy) * (csig * (1.0 + cv * (1.0 - csig)))
    dbuf[0:SPAN, :] = dcv
    vp = vpre[...]
    dv = dcv * chp[3:4, :]
    chg_o[3:4, :] += jnp.sum(dcv * vp, axis=0, keepdims=True)
    chg_o[4:5, :] += jnp.sum(dcv, axis=0, keepdims=True)
    for j in range(1, 4):
        moved = dbuf[j : j + SPAN, :] * aux[:, 8 + j : 9 + j]
        dv = dv + moved * chp[3 - j : 4 - j, :]
        chg_o[3 - j : 4 - j, :] += jnp.sum(moved * vp, axis=0, keepdims=True)
    dbuf[SPAN : SPAN + 8, :] = dbuf[0:8, :]
    vlow = dv.astype(BF16)
    vlow_o[...] = vlow
    heads_o[...] = (
        mm_t(glow[...], wg[...]) + mm_t(vlow, wv[...]) + mm_t(slow, wst[...])
    ).astype(BF16)


def end_kernel(
    dbc, scv_ref, spre, aux_ref, heads, tok, cot, mixed, ng, ws, shp,
    result_o, gtok_o, shlow_o, shg_o, norm_o,
    dbuf,
):
    width = ws.shape[1]

    @pl.when(pl.program_id(0) == 0)
    def _():
        dbuf[SPAN : SPAN + 8, :] = jnp.zeros((8, width), F32)
        shg_o[...] = jnp.zeros_like(shg_o)
        norm_o[...] = jnp.zeros_like(norm_o)

    aux = aux_ref[...]
    scv = scv_ref[...]
    csig = sigmoid(scv)
    dcv = dbc[...] * (csig * (1.0 + scv * (1.0 - csig)))
    dbuf[0:SPAN, :] = dcv
    sp = spre[...]
    ds = dcv * shp[3:4, :]
    shg_o[3:4, :] += jnp.sum(dcv * sp, axis=0, keepdims=True)
    shg_o[4:5, :] += jnp.sum(dcv, axis=0, keepdims=True)
    for j in range(1, 4):
        moved = dbuf[j : j + SPAN, :] * aux[:, 8 + j : 9 + j]
        ds = ds + moved * shp[3 - j : 4 - j, :]
        shg_o[3 - j : 4 - j, :] += jnp.sum(moved * sp, axis=0, keepdims=True)
    dbuf[SPAN : SPAN + 8, :] = dbuf[0:8, :]
    shlow = ds.astype(BF16)
    shlow_o[...] = shlow
    grad_hidden = heads[...].astype(F32) + mm_t(shlow, ws[...])
    x = tok[...].astype(F32)
    inv = lax.rsqrt(jnp.mean(x * x, axis=1, keepdims=True) + EPSILON)
    normed = x * inv
    scaled = grad_hidden * ng[...]
    norm_o[0:1, :] += jnp.sum(grad_hidden * normed, axis=0, keepdims=True)
    mean = jnp.mean(scaled * normed, axis=1, keepdims=True)
    gtok_o[...] = (inv * (scaled - normed * mean) + cot[...].astype(F32)).astype(BF16)
    result_o[...] = (x + mixed[...].astype(F32)).astype(BF16)


def call(body, blocks, ins, outs, scratch, backward, name):
    def spec(shape, kind):
        if kind == "whole":
            return pl.BlockSpec(shape, lambda i: (0,) * len(shape))
        if kind == "lanes":
            block = (shape[0], shape[1] // blocks)
            return pl.BlockSpec(block, (lambda i: (0, blocks - 1 - i)) if backward else (lambda i: (0, i)))
        block = (shape[0] // blocks, shape[1])
        return pl.BlockSpec(block, (lambda i: (blocks - 1 - i, 0)) if backward else (lambda i: (i, 0)))

    return pl.pallas_call(
        body,
        grid=(blocks,),
        in_specs=[spec(a.shape, kind) for a, kind in ins],
        out_specs=[spec(shape, kind) for shape, _, kind in outs],
        out_shape=[jax.ShapeDtypeStruct(shape, dtype) for shape, dtype, _ in outs],
        scratch_shapes=scratch,
        compiler_params=pltpu.CompilerParams(
            dimension_semantics=("arbitrary",), vmem_limit_bytes=60 * 1024 * 1024
        ),
        name=name,
    )(*[a for a, _ in ins])


def pad_rows(parts, width):
    rows = [jnp.pad(p.astype(F32), ((0, 0), (0, width - p.shape[1]))) for p in parts]
    used = sum(r.shape[0] for r in rows)
    return jnp.concatenate(rows + [jnp.zeros((8 - used, width), F32)], axis=0)


def per_device(
    tokens, cotangent, segments, norm_gain, gate_proj, value_proj, shared_proj, step_proj,
    conv_value, bias_value, conv_shared, bias_shared, step_bias, decay_log, skip_gain,
    gate_gain, out_proj,
):
    tp_count = lax.axis_size("tensor")
    length, width = tokens.shape
    inner = gate_proj.shape[1]
    heads = step_proj.shape[1]
    shared_width = shared_proj.shape[1]
    state_size = shared_width // 2
    blocks = length // SPAN
    ids = segments[0]
    back = [jnp.concatenate([jnp.full((j,), -1, ids.dtype), ids[: length - j]]) for j in range(4)]
    ahead = [jnp.concatenate([ids[j:], jnp.full((j,), -1, ids.dtype)]) for j in range(4)]
    ends = ids.reshape(blocks, SPAN)[:, -1]
    before = jnp.concatenate([jnp.full((1,), -1, ids.dtype), ends[:-1]])
    entering = ids == jnp.repeat(before, SPAN)
    leaving = ids == jnp.repeat(ends, SPAN)
    columns = (
        [ids] + [b == ids for b in back[1:]] + [entering, leaving, ids, ids, ids]
        + [a == ids for a in ahead[1:]]
    )
    aux = jnp.stack([c.astype(F32) for c in columns], axis=1)
    segr = ids.astype(F32)[None, :]
    ng = norm_gain[None, :]
    wst = jnp.pad(step_proj, ((0, 0), (0, LANES - heads)))
    chp = pad_rows(
        [conv_value, bias_value[None], gate_gain[None], jnp.repeat(skip_gain, HSIZE)[None]], inner
    )
    shp = pad_rows([conv_shared, bias_shared[None]], shared_width)
    hp = pad_rows([step_bias[None], -jnp.exp(decay_log)[None]], LANES)

    (
        hidden, gate_pre, value_pre, conv_out, shared_pre, shared_conv, z, ld, ldt, yn, sin, gn, stat,
    ) = call(
        fwd_kernel,
        blocks,
        [
            (tokens, "rows"), (cotangent, "rows"), (aux, "rows"), (segr, "lanes"), (ng, "whole"),
            (gate_proj, "whole"), (value_proj, "whole"), (shared_proj, "whole"), (wst, "whole"),
            (out_proj, "whole"), (chp, "whole"), (shp, "whole"), (hp, "whole"),
        ],
        [
            ((length, width), BF16, "rows"),
            ((length, inner), F32, "rows"),
            ((length, inner), F32, "rows"),
            ((length, inner), F32, "rows"),
            ((length, shared_width), F32, "rows"),
            ((length, shared_width), F32, "rows"),
            ((length, LANES), F32, "rows"),
            ((length, LANES), F32, "rows"),
            ((8, length), F32, "lanes"),
            ((length, inner), F32, "rows"),
            ((blocks * state_size, inner), F32, "rows"),
            ((length, inner), F32, "rows"),
            ((8, length), F32, "lanes"),
        ],
        [
            pltpu.VMEM((SPAN + 8, inner), F32),
            pltpu.VMEM((SPAN + 8, shared_width), F32),
            pltpu.VMEM((state_size, inner), F32),
        ],
        False,
        "fwd_scan",
    )
    stat = lax.psum(stat, "tensor")
    total_inner = float(inner * tp_count)

    def gate_body(*refs):
        gate_kernel(total_inner, *refs)

    normal_out, dy, gate_low, gain_part, mixed_part = call(
        gate_body,
        blocks,
        [
            (gate_pre, "rows"), (conv_out, "rows"), (yn, "rows"), (gn, "rows"), (stat, "lanes"),
            (chp, "whole"), (out_proj, "whole"),
        ],
        [
            ((length, inner), BF16, "rows"),
            ((length, inner), F32, "rows"),
            ((length, inner), BF16, "rows"),
            ((8, inner), F32, "whole"),
            ((length, width), BF16, "rows"),
        ],
        [],
        False,
        "gate_step",
    )
    mixed = lax.psum(mixed_part, "tensor")
    early = lax.psum_scatter(
        jnp.concatenate([t_mm(hidden, gate_low), t_mm(cotangent, normal_out)], axis=1).astype(BF16),
        "dp",
        scatter_dimension=0,
        tiled=True,
    ).astype(F32)
    value_low, step_low, dbc, heads_part, ch_grads, head_grads = call(
        bwd_kernel,
        blocks,
        [
            (dy, "rows"), (conv_out, "rows"), (value_pre, "rows"), (shared_conv, "rows"),
            (z, "rows"), (ld, "rows"), (ldt, "lanes"), (yn, "rows"), (sin, "rows"),
            (aux, "rows"), (segr, "lanes"), (gate_low, "rows"), (gate_proj, "whole"),
            (value_proj, "whole"), (wst, "whole"), (chp, "whole"), (hp, "whole"),
        ],
        [
            ((length, inner), BF16, "rows"),
            ((length, LANES), BF16, "rows"),
            ((length, shared_width), F32, "rows"),
            ((length, width), BF16, "rows"),
            ((8, inner), F32, "whole"),
            ((8, LANES), F32, "whole"),
        ],
        [pltpu.VMEM((SPAN + 8, inner), F32), pltpu.VMEM((state_size, inner), F32)],
        True,
        "bwd_scan",
    )
    dbc = lax.psum(dbc, "tensor")
    heads_sum = lax.psum(heads_part, "tensor")
    result, grad_tokens, shared_low, sh_grads, norm_part = call(
        end_kernel,
        blocks,
        [
            (dbc, "rows"), (shared_conv, "rows"), (shared_pre, "rows"), (aux, "rows"),
            (heads_sum, "rows"), (tokens, "rows"), (cotangent, "rows"), (mixed, "rows"),
            (ng, "whole"), (shared_proj, "whole"), (shp, "whole"),
        ],
        [
            ((length, width), BF16, "rows"),
            ((length, width), BF16, "rows"),
            ((length, shared_width), BF16, "rows"),
            ((8, shared_width), F32, "whole"),
            ((8, width), F32, "whole"),
        ],
        [pltpu.VMEM((SPAN + 8, shared_width), F32)],
        True,
        "end_step",
    )
    late = lax.psum_scatter(
        t_mm(hidden, jnp.concatenate([value_low, shared_low, step_low], axis=1)).astype(BF16),
        "dp",
        scatter_dimension=0,
        tiled=True,
    ).astype(F32)
    col_width = width // tp_count
    norm_mine = lax.dynamic_slice_in_dim(
        norm_part[0], lax.axis_index("tensor") * col_width, col_width, 0
    )
    packed = jnp.concatenate(
        [
            norm_mine, ch_grads[:5].reshape(-1), sh_grads[:5].reshape(-1),
            head_grads[:3].reshape(-1), gain_part[0],
        ]
    )
    packed = lax.psum(packed.reshape(-1, LANES), "dp").reshape(-1)
    sizes = [col_width, 5 * inner, 5 * shared_width, 3 * LANES, inner]
    pieces, start = [], 0
    for size in sizes:
        pieces.append(packed[start : start + size])
        start += size
    channel = pieces[1].reshape(5, inner)
    shared = pieces[2].reshape(5, shared_width)
    per_head = pieces[3].reshape(3, LANES)[:, :heads]
    return (
        result,
        grad_tokens,
        pieces[0],
        early[:, :inner],
        late[:, :inner],
        late[:, inner : inner + shared_width],
        late[:, inner + shared_width : inner + shared_width + heads],
        channel[:4],
        channel[4],
        shared[:4],
        shared[4],
        per_head[0],
        per_head[1],
        per_head[2],
        pieces[4],
        early[:, inner:],
    )


def solution(mesh):
    rows, cols, vec = P("dp", None), P(None, "tensor"), P("tensor")
    return jax.shard_map(
        per_device,
        mesh=mesh,
        in_specs=(
            rows, rows, rows, P(), cols, cols, P(), cols, cols, vec, P(), P(), vec, vec, vec, vec, cols,
        ),
        out_specs=(
            rows, rows, vec, P("dp", "tensor"), P("dp", "tensor"), rows, P("dp", "tensor"), cols, vec,
            P(), P(), vec, vec, vec, vec, P("dp", "tensor"),
        ),
        check_vma=False,
    )
```

profile of v0, /device:TPU:0, one launch (start us, length us, event | category | flops | bytes accessed | tf_op | source)
XLA Modules:
  0.0 311.8 jit_solution(17065664800724283749)
XLA Ops:
  8.6 2.0 fusion.18
  11.6 0.8 fusion.20
  12.4 0.8 fusion.19
  15.3 1.1 copy.61.aux_ref
  17.2 0.9 copy.60
  19.6 1.4 maximum_maximum_fusion.shp
  21.0 1.3 fusion.10.hp
  22.3 1.3 concatenate.67.chp.refs_5_
  23.7 19.9 %fwd_scan.1 = (bf16[1024,1024]{1,0:T(8,128)(2,1)}, f32[1024,512]{1,0:T(8,128)}, f32[1024,512]{1,0:T(8,128)}, f32[1024,512]{1,0:T(8,128)}, f32[1024,256]{1,0:T(8,...) custom-call(bf16[1024,1024]{1,0:T(8,128)(2,1)} %tok.3, ...), custom_call_target="tpu_custom_call" | custom-call | tf_op jit(solution)/shard_map/fwd_scan/pallas_call | solution.py:331
  43.6 14.1 %psum.35.refs_4_ = f32[8,1024]{1,0:T(8,128)} all-reduce(f32[8,1024]{1,0:T(8,128)} %get-tuple-element.49), channel_id=1, replica_groups=mesh['dp'=8,'tensor'=4] {'tensor'}, use_global_device_ids=true, to_apply=%region_0.1 | all-reduce | flops 8192 | bytes 65536 | tf_op jit(solution)/shard_map/psum | solution.py:417
  57.8 8.5 %gate_step.1 = (bf16[1024,512]{1,0:T(8,128)(2,1)}, f32[1024,512]{1,0:T(8,128)}, bf16[1024,512]{1,0:T(8,128)(2,1)}, f32[8,512]{1,0:T(8,128)}, bf16[1024,1024]{1,0:T(8,128)(2,1)}) custom-call(f32[1024,512]{1,0:T(8,128)} %get-tuple-element.45.refs_0_, f32[1024,512]{1,0:T(8,128)} %get-tuple-element.46.refs_1_.cv_ref, f32[1024,512]{1,0:T(8,128)} %get-tuple-element.47.refs_2_.yn, ...), custom_call_target="tpu_custom_call" | custom-call | tf_op jit(solution)/shard_map/gate_step/pallas_call | solution.py:331
  66.3 26.7 %bwd_scan.1 = (bf16[1024,512]{1,0:T(8,128)(2,1)}, bf16[1024,128]{1,0:T(8,128)(2,1)}, f32[1024,256]{1,0:T(8,128)}, bf16[1024,1024]{1,0:T(8,128)(2,1)}, f32[8,512]{1,0:T(8,128)}, /*index=5*/f32[8,128]{1,0:T(8,128)}) custom-call(f32[1024,512]{1,0:T(8,128)} %get-tuple-element.50.dy_ref, f32[1024,512]{1,0:T(8,128)} %get-tuple-element.46.refs_1_.cv_ref, ...), custom_call_target="tpu_custom_call" | custom-call | tf_op jit(solution)/shard_map/bwd_scan/pallas_call | solution.py:331
  94.9 1.3 convolution_convert_fusion.1
  96.8 1.3 fusion.9
  98.2 2.6 copy.67
  100.9 29.1 %all-reduce.11.cloned.1.call-done.dbc = f32[1024,256]{1,0:T(8,128)} async-done(((f32[1024,256]{1,0:T(8,128)}), f32[1024,256]{1,0:T(8,128)}) %all-reduce.11.cloned.1.call-update) | async-done | bytes 1048592 | tf_op jit(solution)/shard_map/psum | solution.py:469
  130.0 88.8 %all-reduce.13.cloned.1.call-done = (bf16[1024,1024]{1,0:T(8,128)(2,1)}, bf16[1024,1024]{1,0:T(8,128)(2,1)}) async-done(((bf16[1024,1024]{1,0:T(8,128)(2,1)}, bf16[1024,1024]{1,0:T(8,128)(2,1)}), (bf16[1024,1024]{1,0:T(8,128)(2,1)}, bf16[1024,1024]{1,0:T(8,128)(2,1)})) %all-reduce.13.cloned.1.call-update) | async-done | bytes 4194320 | tf_op jit(solution)/shard_map/psum | solution.py:470
  218.8 9.2 %end_step.1 = (bf16[1024,1024]{1,0:T(8,128)(2,1)}, bf16[1024,1024]{1,0:T(8,128)(2,1)}, bf16[1024,256]{1,0:T(8,128)(2,1)}, f32[8,256]{1,0:T(8,128)}, f32[8,1024]{1,0:T(8,128)}) custom-call(f32[1024,256]{1,0:T(8,128)} %all-reduce.11.cloned.1.call-done.dbc, f32[1024,256]{1,0:T(8,128)} %get-tuple-element.52.scv_ref, f32[1024,256]{1,0:T(8,128)} %get-tuple-element.59.spre, ...), custom_call_target="tpu_custom_call" | custom-call | tf_op jit(solution)/shard_map/end_step/pallas_call | solution.py:331
  228.1 4.7 %fusion.6 = bf16[1024,896]{1,0:T(8,128)(2,1)} fusion(bf16[1024,1024]{1,0:T(8,128)(2,1)S(1)} %copy-done.7, bf16[1024,128]{1,0:T(8,128)(2,1)S(1)} %copy-done.9, bf16[1024,256]{1,0:T(8,128)(2,1)} %get-tuple-element.72, bf16[1024,512]{1,0:T(8,128)(2,1)S(1)} %copy-done.8), kind=kOutput, calls=%fused_computation.7 | convolution fusion | flops 1885470720 | bytes 5767168 | tf_op jit(solution)/shard_map/dot_general | solution.py:27
  234.4 37.2 %psum.39 = f32[39,128]{1,0:T(8,128)S(1)} all-reduce(f32[39,128]{1,0:T(8,128)S(1)} %bitcast.68), channel_id=1, replica_groups=mesh['dp'=8,'tensor'=4] {'dp'}, use_global_device_ids=true, to_apply=%region_4.5 | all-reduce | flops 4992 | bytes 39936 | tf_op jit(solution)/shard_map/psum | solution.py:506
  274.6 1.1 copy.68
  277.4 22.4 %reduce-scatter.5.cloned.1.call-done = bf16[128,896]{1,0:T(8,128)(2,1)} async-done(((bf16[1024,896]{1,0:T(8,128)(2,1)}), bf16[128,896]{1,0:T(8,128)(2,1)}) %reduce-scatter.5.cloned.1.call-update) | async-done | bytes 229392 | tf_op jit(solution)/shard_map/reduce_scatter | solution.py:490
  301.2 1.6 slice.170
  302.9 1.5 slice.171
  (77 shorter events, 16.3 us)
Async XLA Ops:
  8.0 122.0 %all-reduce.11.cloned.1.call-start = ((), (), s32[]{:S(2)}) async-start(), calls=%async_computation.2 | async-start | bytes 2097152 | tf_op jit(solution)/shard_map/psum | solution.py:469
  93.0 125.8 %all-reduce.13.cloned.1.call-start = ((), (), s32[]{:S(2)}) async-start(), calls=%async_computation.5 | async-start | bytes 8388608 | tf_op jit(solution)/shard_map/psum | solution.py:470
  93.0 1.2 copy-start.1
  93.0 1.9 copy-start.6
  93.7 180.8 %reduce-scatter.7.cloned.1.call-start = ((), (), s32[]{:S(2)}) async-start(), calls=%async_computation.4 | async-start | bytes 2359296
  94.9 1.6 copy-start
  94.9 1.9 copy-start.2
  100.9 199.0 %reduce-scatter.5.cloned.1.call-start = ((), (), s32[]{:S(2)}) async-start(), calls=%async_computation.3 | async-start | bytes 2064384 | tf_op jit(solution)/shard_map/reduce_scatter | solution.py:490
  218.8 9.2 %copy-start.7 = (bf16[1024,1024]{1,0:T(8,128)(2,1)S(1)}, bf16[1024,1024]{1,0:T(8,128)(2,1)}, u32[]{:S(2)}) copy-start(bf16[1024,1024]{1,0:T(8,128)(2,1)} %get-tuple-element.69) | copy-start | bytes 6291460
  218.8 9.2 %copy-start.8 = (bf16[1024,512]{1,0:T(8,128)(2,1)S(1)}, bf16[1024,512]{1,0:T(8,128)(2,1)}, u32[]{:S(2)}) copy-start(bf16[1024,512]{1,0:T(8,128)(2,1)} %get-tuple-element.71) | copy-start | bytes 3145732
  218.8 9.3 %copy-start.9 = (bf16[1024,128]{1,0:T(8,128)(2,1)S(1)}, bf16[1024,128]{1,0:T(8,128)(2,1)}, u32[]{:S(2)}) copy-start(bf16[1024,128]{1,0:T(8,128)(2,1)} %get-tuple-element.73) | copy-start | bytes 786436
  228.0 4.8 %copy-start.3 = (f32[8,512]{1,0:T(8,128)S(1)}, f32[8,512]{1,0:T(8,128)}, u32[]{:S(2)}) copy-start(f32[8,512]{1,0:T(8,128)} %get-tuple-element.65) | copy-start | bytes 49156
  228.0 6.3 %copy-start.4 = (f32[8,256]{1,0:T(8,128)S(1)}, f32[8,256]{1,0:T(8,128)}, u32[]{:S(2)}) copy-start(f32[8,256]{1,0:T(8,128)} %get-tuple-element.66) | copy-start | bytes 24580
  228.0 6.3 %copy-start.5 = (f32[8,128]{1,0:T(8,128)S(1)}, f32[8,128]{1,0:T(8,128)}, u32[]{:S(2)}) copy-start(f32[8,128]{1,0:T(8,128)} %get-tuple-element.67) | copy-start | bytes 12292
Sparse Core Ops, SparseCore 0:
  93.1 36.8 all-reduce.10
  133.0 85.6 all-reduce.12
Sparse Core Ops, SparseCore 1:
  100.9 68.8 reduce-scatter.6
  232.9 66.9 reduce-scatter.4
where the time goes:
time: 313 us; the launch traced here: 312 us
  waiting for transfers between devices  141 us (45%)
  Pallas kernels  64.3 us (21%)
  blocking collectives  51.4 us (16%)
  local copies, waits for them, and re-layouts  24.6 us (8%)
  between operations  15.8 us (5%)
  matrix products  7.29 us (2%)
  other arithmetic  7.14 us (2%)
    psum x1, waiting for transfers between devices, per_device(): heads_sum = lax.psum(heads_part, 'tensor')  88.8 us
    pallas_call x4, Pallas kernels, call(): pl.pallas_call(body, grid=(blocks,), in_specs=[spec(a.shape, kind) for a,...  64.3 us
    psum x1, blocking collectives, per_device(): packed = lax.psum(packed.reshape(-1, LANES), 'dp').reshape(-1)  37.2 us
    psum x1, waiting for transfers between devices, per_device(): dbc = lax.psum(dbc, 'tensor')  29.1 us
    reduce_scatter x1, waiting for transfers between devices, per_device(): lax.psum_scatter(t_mm(hidden, jnp.concatenate([value_low, shared_low, ste...  22.4 us
    psum x1, blocking collectives, per_device(): stat = lax.psum(stat, 'tensor')  14.1 us
    unnamed x37, local copies, waits for them, and re-layouts  9.38 us
    dot_general x3, matrix products, t_mm(): lax.dot_general(left, right, (((0,), (0,)), ((), ())), preferred_element_...  7.29 us
  transfers between devices with their start and end apart: 4, of which 3 were waited for; matrix products, arithmetic and copies ran while one was open for 6% of the time, Pallas kernels for 3%

commit v1 on v0

--- a/solution.py
+++ b/solution.py
@@ -174,7 +174,7 @@
 def bwd_kernel(
     dy_ref, cv_ref, vpre, scv_ref, z_ref, ld_ref, ldt_ref, yn, sin, aux_ref, segr, glow,
     wg, wv, wst, chp, hp,
-    vlow_o, slow_o, dbc_o, heads_o, chg_o, hg_o,
+    vlow_o, slow_o, heads_o, chg_o, hg_o,
     dbuf, dstate,
 ):
     inner = wg.shape[1]
@@ -237,7 +237,6 @@
     xse_low = (xs * eout_x).astype(BF16)
     db = mm(dscores_low, c_low) + mm_t(xse_low, dst_low)
     dc = t_mm(dscores_low, b_low) + mm_t(dye_low, old.astype(BF16))
-    dbc_o[...] = jnp.concatenate([db, dc], axis=1)
     late = mm(b_low, dst_low) * eout_x
     keep = ein_x[SPAN - 1 : SPAN, :]
     dstate[...] = dst * keep + t_mm(c_low, dye_low)
@@ -273,14 +272,13 @@
     dbuf[SPAN : SPAN + 8, :] = dbuf[0:8, :]
     vlow = dv.astype(BF16)
     vlow_o[...] = vlow
-    heads_o[...] = (
-        mm_t(glow[...], wg[...]) + mm_t(vlow, wv[...]) + mm_t(slow, wst[...])
-    ).astype(BF16)
+    back = mm_t(glow[...], wg[...]) + mm_t(vlow, wv[...]) + mm_t(slow, wst[...])
+    heads_o[...] = jnp.concatenate([back, db, dc], axis=1).astype(BF16)
 
 
 def end_kernel(
-    dbc, scv_ref, spre, aux_ref, heads, tok, cot, mixed, ng, ws, shp,
-    result_o, gtok_o, shlow_o, shg_o, norm_o,
+    summed, scv_ref, spre, aux_ref, tok, cot, ng, ws, shp,
+    gtok_o, shlow_o, shg_o, norm_o,
     dbuf,
 ):
     width = ws.shape[1]
@@ -294,7 +292,7 @@
     aux = aux_ref[...]
     scv = scv_ref[...]
     csig = sigmoid(scv)
-    dcv = dbc[...] * (csig * (1.0 + scv * (1.0 - csig)))
+    dcv = summed[:, tok.shape[1] :].astype(F32) * (csig * (1.0 + scv * (1.0 - csig)))
     dbuf[0:SPAN, :] = dcv
     sp = spre[...]
     ds = dcv * shp[3:4, :]
@@ -307,7 +305,7 @@
     dbuf[SPAN : SPAN + 8, :] = dbuf[0:8, :]
     shlow = ds.astype(BF16)
     shlow_o[...] = shlow
-    grad_hidden = heads[...].astype(F32) + mm_t(shlow, ws[...])
+    grad_hidden = summed[:, : tok.shape[1]].astype(F32) + mm_t(shlow, ws[...])
     x = tok[...].astype(F32)
     inv = lax.rsqrt(jnp.mean(x * x, axis=1, keepdims=True) + EPSILON)
     normed = x * inv
@@ -315,7 +313,173 @@
     norm_o[0:1, :] += jnp.sum(grad_hidden * normed, axis=0, keepdims=True)
     mean = jnp.mean(scaled * normed, axis=1, keepdims=True)
     gtok_o[...] = (inv * (scaled - normed * mean) + cot[...].astype(F32)).astype(BF16)
-    result_o[...] = (x + mixed[...].astype(F32)).astype(BF16)
+
+
+MESH = pl.DeviceIdType.MESH
+PIECES = 4
+
+
+def prep_kernel(seg, aux_o, segr_o):
+    length = seg.shape[1]
+    ids = seg[...].astype(F32)
+    segr_o[...] = ids
+    wide = ids + jnp.zeros((8, length), F32)
+    lane = lax.broadcasted_iota(jnp.int32, (8, length), 1)
+    row = lax.broadcasted_iota(jnp.int32, (8, length), 0)
+    ends = [
+        ids[:, start + SPAN - 1 : start + SPAN] + jnp.zeros((8, SPAN), F32)
+        for start in range(0, length, SPAN)
+    ]
+    last = jnp.concatenate(ends, axis=1)
+    before = jnp.concatenate([jnp.full((8, SPAN), -1.0, F32)] + ends[:-1], axis=1)
+    first = jnp.where(row == 0, wide, 0.0)
+    first = jnp.where((row == 4) & (wide == before), 1.0, first)
+    first = jnp.where((row == 5) & (wide == last), 1.0, first)
+    second = jnp.zeros((8, length), F32)
+    for j in range(1, 4):
+        back = (pltpu.roll(wide, j, 1) == wide) & (lane >= j)
+        ahead = (pltpu.roll(wide, length - j, 1) == wide) & (lane < length - j)
+        first = jnp.where((row == j) & back, 1.0, first)
+        second = jnp.where((row == j) & ahead, 1.0, second)
+    rest = jnp.zeros((LANES - 16, length), F32)
+    aux_o[...] = jnp.transpose(jnp.concatenate([first, second, rest], axis=0))
+
+
+def small_sum(x, axis, collective_id):
+    count = lax.axis_size(axis)
+
+    def body(x_ref, out_ref, slots, send, recv):
+        me = lax.axis_index(axis)
+        barrier = pltpu.get_barrier_semaphore()
+        for k in range(1, count):
+            peer = lax.rem(me + k, count)
+            pl.semaphore_signal(barrier, inc=1, device_id={axis: peer}, device_id_type=MESH)
+        pl.semaphore_wait(barrier, count - 1)
+        copies = []
+        for k in range(1, count):
+            copies.append(
+                pltpu.make_async_remote_copy(
+                    src_ref=x_ref,
+                    dst_ref=slots.at[k],
+                    send_sem=send.at[k],
+                    recv_sem=recv.at[k],
+                    device_id={axis: lax.rem(me + k, count)},
+                    device_id_type=MESH,
+                )
+            )
+            copies[-1].start()
+        slots[0] = x_ref[...]
+        for copy in copies:
+            copy.wait()
+        total = slots[me]
+        for source in range(1, count):
+            total = total + slots[lax.rem(me - source + count, count)]
+        out_ref[...] = total
+
+    return pl.pallas_call(
+        body,
+        in_specs=[pl.BlockSpec(memory_space=pltpu.VMEM)],
+        out_specs=pl.BlockSpec(memory_space=pltpu.VMEM),
+        out_shape=jax.ShapeDtypeStruct(x.shape, x.dtype),
+        scratch_shapes=[
+            pltpu.VMEM((count,) + x.shape, x.dtype),
+            pltpu.SemaphoreType.DMA((count,)),
+            pltpu.SemaphoreType.DMA((count,)),
+        ],
+        compiler_params=pltpu.CompilerParams(collective_id=collective_id, has_side_effects=True),
+        name="small_sum_" + axis,
+    )(x)
+
+
+def wide_sum(x, axis, collective_id):
+    groups = lax.axis_size(axis) // 2
+    length, width = x.shape
+    half = length // 2
+    rows = half // PIECES
+
+    def body(x_ref, out_ref, near, far, send_a, recv_a, send_b, recv_b, send_c, recv_c):
+        me = lax.axis_index(axis)
+        side = lax.rem(me, 2)
+        chip = me // 2
+        sibling = 2 * chip + 1 - side
+        mates = [2 * lax.rem(chip + q, groups) + side for q in range(1, groups)]
+        barrier = pltpu.get_barrier_semaphore()
+        for peer in [sibling] + mates:
+            pl.semaphore_signal(barrier, inc=1, device_id={axis: peer}, device_id_type=MESH)
+        pl.semaphore_wait(barrier, groups)
+        first, second, third = [], [], []
+
+        def part(which, k):
+            return pl.ds(pl.multiple_of(which * half + k * rows, rows), rows)
+
+        for k in range(PIECES):
+            first.append(
+                pltpu.make_async_remote_copy(
+                    src_ref=x_ref.at[part(1 - side, k)],
+                    dst_ref=near.at[k],
+                    send_sem=send_a.at[k],
+                    recv_sem=recv_a.at[k],
+                    device_id={axis: sibling},
+                    device_id_type=MESH,
+                )
+            )
+            first[-1].start()
+        for k in range(PIECES):
+            first[k].wait_recv()
+            mine = x_ref[part(side, k), :].astype(F32) + near[k].astype(F32)
+            far[0, k] = mine.astype(BF16)
+            for q in range(1, groups):
+                second.append(
+                    pltpu.make_async_remote_copy(
+                        src_ref=far.at[0, k],
+                        dst_ref=far.at[q, k],
+                        send_sem=send_b.at[q, k],
+                        recv_sem=recv_b.at[q, k],
+                        device_id={axis: mates[q - 1]},
+                        device_id_type=MESH,
+                    )
+                )
+                second[-1].start()
+        for k in range(PIECES):
+            for q in range(1, groups):
+                second[k * (groups - 1) + q - 1].wait_recv()
+            total = far[chip, k].astype(F32)
+            for source in range(1, groups):
+                total = total + far[lax.rem(chip - source + groups, groups), k].astype(F32)
+            out_ref[part(side, k), :] = total.astype(BF16)
+            third.append(
+                pltpu.make_async_remote_copy(
+                    src_ref=out_ref.at[part(side, k)],
+                    dst_ref=out_ref.at[part(side, k)],
+                    send_sem=send_c.at[k],
+                    recv_sem=recv_c.at[k],
+                    device_id={axis: sibling},
+                    device_id_type=MESH,
+                )
+            )
+            third[-1].start()
+        for copy in first + second:
+            copy.wait_send()
+        for copy in third:
+            copy.wait()
+
+    dma = pltpu.SemaphoreType.DMA
+    return pl.pallas_call(
+        body,
+        in_specs=[pl.BlockSpec(memory_space=pltpu.VMEM)],
+        out_specs=pl.BlockSpec(memory_space=pltpu.VMEM),
+        out_shape=jax.ShapeDtypeStruct(x.shape, x.dtype),
+        scratch_shapes=[
+            pltpu.VMEM((PIECES, rows, width), BF16),
+            pltpu.VMEM((groups, PIECES, rows, width), BF16),
+            dma((PIECES,)), dma((PIECES,)), dma((groups, PIECES)), dma((groups, PIECES)),
+            dma((PIECES,)), dma((PIECES,)),
+        ],
+        compiler_params=pltpu.CompilerParams(
+            collective_id=collective_id, has_side_effects=True, vmem_limit_bytes=40 * 1024 * 1024
+        ),
+        name="wide_sum",
+    )(x)
 
 
 def call(body, blocks, ins, outs, scratch, backward, name):
@@ -360,19 +524,14 @@
     shared_width = shared_proj.shape[1]
     state_size = shared_width // 2
     blocks = length // SPAN
-    ids = segments[0]
-    back = [jnp.concatenate([jnp.full((j,), -1, ids.dtype), ids[: length - j]]) for j in range(4)]
-    ahead = [jnp.concatenate([ids[j:], jnp.full((j,), -1, ids.dtype)]) for j in range(4)]
-    ends = ids.reshape(blocks, SPAN)[:, -1]
-    before = jnp.concatenate([jnp.full((1,), -1, ids.dtype), ends[:-1]])
-    entering = ids == jnp.repeat(before, SPAN)
-    leaving = ids == jnp.repeat(ends, SPAN)
-    columns = (
-        [ids] + [b == ids for b in back[1:]] + [entering, leaving, ids, ids, ids]
-        + [a == ids for a in ahead[1:]]
-    )
-    aux = jnp.stack([c.astype(F32) for c in columns], axis=1)
-    segr = ids.astype(F32)[None, :]
+    aux, segr = pl.pallas_call(
+        prep_kernel,
+        out_shape=[
+            jax.ShapeDtypeStruct((length, LANES), F32),
+            jax.ShapeDtypeStruct((1, length), F32),
+        ],
+        name="prep_step",
+    )(segments)
     ng = norm_gain[None, :]
     wst = jnp.pad(step_proj, ((0, 0), (0, LANES - heads)))
     chp = pad_rows(
@@ -414,7 +573,7 @@
         False,
         "fwd_scan",
     )
-    stat = lax.psum(stat, "tensor")
+    stat = small_sum(stat, "tensor", 0)
     total_inner = float(inner * tp_count)
 
     def gate_body(*refs):
@@ -439,45 +598,48 @@
         "gate_step",
     )
     mixed = lax.psum(mixed_part, "tensor")
+    value_low, step_low, heads_part, ch_grads, head_grads = call(
+        bwd_kernel,
+        blocks,
+        [
+            (dy, "rows"), (conv_out, "rows"), (value_pre, "rows"), (shared_conv, "rows"),
+            (z, "rows"), (ld, "rows"), (ldt, "lanes"), (yn, "rows"), (sin, "rows"),
+            (aux, "rows"), (segr, "lanes"), (gate_low, "rows"), (gate_proj, "whole"),
+            (value_proj, "whole"), (wst, "whole"), (chp, "whole"), (hp, "whole"),
+        ],
+        [
+            ((length, inner), BF16, "rows"),
+            ((length, LANES), BF16, "rows"),
+            ((length, width + shared_width), BF16, "rows"),
+            ((8, inner), F32, "whole"),
+            ((8, LANES), F32, "whole"),
+        ],
+        [pltpu.VMEM((SPAN + 8, inner), F32), pltpu.VMEM((state_size, inner), F32)],
+        True,
+        "bwd_scan",
+    )
     early = lax.psum_scatter(
-        jnp.concatenate([t_mm(hidden, gate_low), t_mm(cotangent, normal_out)], axis=1).astype(BF16),
+        jnp.concatenate(
+            [
+                t_mm(hidden, jnp.concatenate([gate_low, value_low, step_low], axis=1)),
+                t_mm(cotangent, normal_out),
+            ],
+            axis=1,
+        ).astype(BF16),
         "dp",
         scatter_dimension=0,
         tiled=True,
     ).astype(F32)
-    value_low, step_low, dbc, heads_part, ch_grads, head_grads = call(
-        bwd_kernel,
-        blocks,
-        [
-            (dy, "rows"), (conv_out, "rows"), (value_pre, "rows"), (shared_conv, "rows"),
-            (z, "rows"), (ld, "rows"), (ldt, "lanes"), (yn, "rows"), (sin, "rows"),
-            (aux, "rows"), (segr, "lanes"), (gate_low, "rows"), (gate_proj, "whole"),
-            (value_proj, "whole"), (wst, "whole"), (chp, "whole"), (hp, "whole"),
-        ],
-        [
-            ((length, inner), BF16, "rows"),
-            ((length, LANES), BF16, "rows"),
-            ((length, shared_width), F32, "rows"),
-            ((length, width), BF16, "rows"),
-            ((8, inner), F32, "whole"),
-            ((8, LANES), F32, "whole"),
-        ],
-        [pltpu.VMEM((SPAN + 8, inner), F32), pltpu.VMEM((state_size, inner), F32)],
-        True,
-        "bwd_scan",
-    )
-    dbc = lax.psum(dbc, "tensor")
-    heads_sum = lax.psum(heads_part, "tensor")
-    result, grad_tokens, shared_low, sh_grads, norm_part = call(
+    summed = wide_sum(heads_part, "tensor", 1)
+    grad_tokens, shared_low, sh_grads, norm_part = call(
         end_kernel,
         blocks,
         [
-            (dbc, "rows"), (shared_conv, "rows"), (shared_pre, "rows"), (aux, "rows"),
-            (heads_sum, "rows"), (tokens, "rows"), (cotangent, "rows"), (mixed, "rows"),
+            (summed, "rows"), (shared_conv, "rows"), (shared_pre, "rows"), (aux, "rows"),
+            (tokens, "rows"), (cotangent, "rows"),
             (ng, "whole"), (shared_proj, "whole"), (shp, "whole"),
         ],
         [
-            ((length, width), BF16, "rows"),
             ((length, width), BF16, "rows"),
             ((length, shared_width), BF16, "rows"),
             ((8, shared_width), F32, "whole"),
@@ -488,7 +650,7 @@
         "end_step",
     )
     late = lax.psum_scatter(
-        t_mm(hidden, jnp.concatenate([value_low, shared_low, step_low], axis=1)).astype(BF16),
+        t_mm(hidden, shared_low).astype(BF16),
         "dp",
         scatter_dimension=0,
         tiled=True,
@@ -503,7 +665,9 @@
             head_grads[:3].reshape(-1), gain_part[0],
         ]
     )
-    packed = lax.psum(packed.reshape(-1, LANES), "dp").reshape(-1)
+    packed = packed.reshape(-1, LANES)
+    packed = jnp.pad(packed, ((0, -packed.shape[0] % 8), (0, 0)))
+    packed = small_sum(packed, "dp", 2).reshape(-1)
     sizes = [col_width, 5 * inner, 5 * shared_width, 3 * LANES, inner]
     pieces, start = [], 0
     for size in sizes:
@@ -512,14 +676,15 @@
     channel = pieces[1].reshape(5, inner)
     shared = pieces[2].reshape(5, shared_width)
     per_head = pieces[3].reshape(3, LANES)[:, :heads]
+    result = (tokens.astype(F32) + mixed.astype(F32)).astype(BF16)
     return (
         result,
         grad_tokens,
         pieces[0],
         early[:, :inner],
-        late[:, :inner],
-        late[:, inner : inner + shared_width],
-        late[:, inner + shared_width : inner + shared_width + heads],
+        early[:, inner : 2 * inner],
+        late,
+        early[:, 2 * inner : 2 * inner + heads],
         channel[:4],
         channel[4],
         shared[:4],
@@ -528,7 +693,7 @@
         per_head[1],
         per_head[2],
         pieces[4],
-        early[:, inner:],
+        early[:, 2 * inner + LANES :],
     )
 
 

time: 313 us -> 285 us (0.911)
  Pallas kernels: 64.3 us -> 117 us
  blocking collectives: 51.4 us -> 0 us
  waiting for transfers between devices: 141 us -> 111 us
  other arithmetic: 7.14 us -> 10.8 us
  local copies, waits for them, and re-layouts: 24.6 us -> 21.2 us
    psum x2 -> x1, waiting for transfers between devices: 118 us -> 0.01 us  [per_device(): mixed = lax.psum(mixed_part, 'tensor')]
    reduce_scatter x1 -> x2, waiting for transfers between devices: 22.4 us -> 111 us  [the longest x1 75.1 us: per_device(): lax.psum_scatter(jnp.concatenate([t_mm(hidden, jnp.concatenate([gate_low,...]
    pallas_call x0 -> x4, Pallas kernels: none -> 53.5 us  [the longest x1 34.3 us: wide_sum(): pl.pallas_call(body, in_specs=[pl.BlockSpec(memory_space=pltpu.VMEM)], ou...]
    psum x2 -> x0, blocking collectives: 51.4 us -> none  [the longest x1 37.2 us: per_device(): packed = lax.psum(packed.reshape(-1, LANES), 'dp').reshape(-1)]
    unnamed x37 -> x32, local copies, waits for them, and re-layouts: 9.38 us -> 6.71 us
  transfers between devices with their start and end apart: 4 -> 3, of which waited for: 3 -> 2; matrix products, arithmetic and copies ran while one was open for 6% -> 7% of each run, Pallas kernels for 3% -> 4%
where the time goes in v1:
time: 285 us; the launch traced here: 283 us
  Pallas kernels  117 us (41%)
  waiting for transfers between devices  111 us (39%)
  local copies, waits for them, and re-layouts  21.2 us (7%)
  between operations  15.7 us (6%)
  other arithmetic  10.8 us (4%)
  matrix products  7.17 us (3%)
    reduce_scatter x1, waiting for transfers between devices, per_device(): lax.psum_scatter(jnp.concatenate([t_mm(hidden, jnp.concatenate([gate_low,...  75.1 us
    pallas_call x4, Pallas kernels, call(): pl.pallas_call(body, grid=(blocks,), in_specs=[spec(a.shape, kind) for a,...  63.6 us
    reduce_scatter x1, waiting for transfers between devices, per_device(): lax.psum_scatter(t_mm(hidden, shared_low).astype(BF16), 'dp', scatter_dim...  35.8 us
    pallas_call x1, Pallas kernels, wide_sum(): pl.pallas_call(body, in_specs=[pl.BlockSpec(memory_space=pltpu.VMEM)], ou...  34.3 us
    pallas_call x2, Pallas kernels, small_sum(): pl.pallas_call(body, in_specs=[pl.BlockSpec(memory_space=pltpu.VMEM)], ou...  17.4 us
    dot_general x3, matrix products, t_mm(): lax.dot_general(left, right, (((0,), (0,)), ((), ())), preferred_element_...  7.17 us
    unnamed x32, local copies, waits for them, and re-layouts  6.71 us
  transfers between devices with their start and end apart: 3, of which 2 were waited for; matrix products, arithmetic and copies ran while one was open for 7% of the time, Pallas kernels for 4%

profile of v1, /device:TPU:0, one launch (start us, length us, event | category | flops | bytes accessed | tf_op | source)
XLA Modules:
  0.0 283.5 jit_solution(17660530288862502705)
XLA Ops:
  8.1 1.8 prep_step.1
  13.1 1.4 maximum_maximum_fusion.shp
  14.5 1.3 fusion.6.hp
  15.8 1.3 concatenate.19.chp.refs_5_
  17.2 19.9 %fwd_scan.1 = (bf16[1024,1024]{1,0:T(8,128)(2,1)}, f32[1024,512]{1,0:T(8,128)}, f32[1024,512]{1,0:T(8,128)}, f32[1024,512]{1,0:T(8,128)}, f32[1024,256]{1,0:T(8,...) custom-call(bf16[1024,1024]{1,0:T(8,128)(2,1)} %tok.3, ...), custom_call_target="tpu_custom_call" | custom-call | tf_op jit(solution)/shard_map/fwd_scan/pallas_call | solution.py:495
  37.1 6.7 %small_sum_tensor.1.refs_4_ = f32[8,1024]{1,0:T(8,128)} custom-call(f32[8,1024]{1,0:T(8,128)} %get-tuple-element.51.x_ref), custom_call_target="tpu_custom_call" | custom-call | tf_op jit(solution)/shard_map/small_sum_tensor/pallas_call | solution.py:379
  43.8 8.5 %gate_step.1 = (bf16[1024,512]{1,0:T(8,128)(2,1)}, f32[1024,512]{1,0:T(8,128)}, bf16[1024,512]{1,0:T(8,128)(2,1)}, f32[8,512]{1,0:T(8,128)}, bf16[1024,1024]{1,0:T(8,128)(2,1)}) custom-call(f32[1024,512]{1,0:T(8,128)} %get-tuple-element.47.refs_0_, f32[1024,512]{1,0:T(8,128)} %get-tuple-element.48.refs_1_.cv_ref, f32[1024,512]{1,0:T(8,128)} %get-tuple-element.49.refs_2_.yn, ...), custom_call_target="tpu_custom_call" | custom-call | tf_op jit(solution)/shard_map/gate_step/pallas_call | solution.py:495
  52.3 26.7 %bwd_scan.1 = (bf16[1024,512]{1,0:T(8,128)(2,1)}, bf16[1024,128]{1,0:T(8,128)(2,1)}, bf16[1024,1280]{1,0:T(8,128)(2,1)}, f32[8,512]{1,0:T(8,128)}, f32[8,128]{1,0:T(8,128)}) custom-call(f32[1024,512]{1,0:T(8,128)} %get-tuple-element.53.dy_ref, f32[1024,512]{1,0:T(8,128)} %get-tuple-element.48.refs_1_.cv_ref, f32[1024,512]{1,0:T(8,128)} %get-tuple-element.54.vpre, ...), custom_call_target="tpu_custom_call" | custom-call | tf_op jit(solution)/shard_map/bwd_scan/pallas_call | solution.py:495
  79.1 1.7 copy-done.1
  80.8 34.3 %wide_sum.1.summed = bf16[1024,1280]{1,0:T(8,128)(2,1)S(1)} custom-call(bf16[1024,1280]{1,0:T(8,128)(2,1)S(1)} %copy-done.1), custom_call_target="tpu_custom_call" | custom-call | tf_op jit(solution)/shard_map/wide_sum/pallas_call | solution.py:467
  115.1 1.6 copy-done
  116.7 8.4 %end_step.1 = (bf16[1024,1024]{1,0:T(8,128)(2,1)}, bf16[1024,256]{1,0:T(8,128)(2,1)}, f32[8,256]{1,0:T(8,128)}, f32[8,1024]{1,0:T(8,128)}) custom-call(bf16[1024,1280]{1,0:T(8,128)(2,1)} %copy-done, f32[1024,256]{1,0:T(8,128)} %get-tuple-element.55.scv_ref, f32[1024,256]{1,0:T(8,128)} %get-tuple-element.62.spre, f32[1024,128]{1,0:T(8,128)} %get-tuple-element.45.aux_ref, ...), custom_call_target="tpu_custom_call" | custom-call | tf_op jit(solution)/shard_map/end_step/pallas_call | solution.py:495
  125.1 2.7 convolution_convert_fusion.2
  129.4 1.3 fusion.5
  131.6 3.2 %convolution_convert_fusion = bf16[1024,1152]{1,0:T(8,128)(2,1)S(1)} fusion(bf16[1024,1024]{1,0:T(8,128)(2,1)S(1)} %copy-done.9, bf16[1024,128]{1,0:T(8,128)(2,1)S(1)} %copy-done.12, bf16[1024,512]{1,0:T(8,128)(2,1)S(1)} %copy-done.11, bf16[1024,512]{1,0:T(8,128)(2,1)S(1)} %copy-done.4), kind=kOutput, calls=%fused_computation.1 | convolution fusion | flops 2424176640 | bytes 6815744 | tf_op jit(solution)/shard_map/dot_general | solution.py:27
  134.8 2.1 pad_maximum_fusion
  139.2 10.7 %small_sum_dp.1 = f32[40,128]{1,0:T(8,128)} custom-call(f32[40,128]{1,0:T(8,128)} %pad.18.x_ref), custom_call_target="tpu_custom_call" | custom-call | tf_op jit(solution)/shard_map/small_sum_dp/pallas_call | solution.py:379
  152.5 1.3 slice_bitcast_fusion.4
  155.1 1.3 slice_bitcast_fusion
  156.4 35.8 %reduce-scatter.5.cloned.1.call-done = bf16[128,256]{1,0:T(8,128)(2,1)} async-done(((bf16[1024,256]{1,0:T(8,128)(2,1)}), bf16[128,256]{1,0:T(8,128)(2,1)}) %reduce-scatter.5.cloned.1.call-update) | async-done | bytes 65552 | tf_op jit(solution)/shard_map/reduce_scatter | solution.py:652
  192.2 1.5 convert_element_type.31
  193.7 3.9 %add_convert_fusion = bf16[1024,1024]{1,0:T(8,128)(2,1)} fusion(bf16[1024,1024]{1,0:T(8,128)(2,1)} %all-reduce.6.cloned.1.call-done, bf16[1024,1024]{1,0:T(8,128)(2,1)S(1)} %copy-done.2), kind=kLoop, calls=%fused_computation | loop fusion | flops 4194304 | bytes 6291456 | tf_op jit(solution)/shard_map/convert_element_type | solution.py:679
  197.5 75.1 %reduce-scatter.3.cloned.1.call-done = bf16[128,1664]{1,0:T(8,128)(2,1)} async-done(((bf16[1024,1664]{1,0:T(8,128)(2,1)}), bf16[128,1664]{1,0:T(8,128)(2,1)}) %reduce-scatter.3.cloned.1.call-update) | async-done | bytes 426000 | tf_op jit(solution)/shard_map/reduce_scatter | solution.py:621
  274.1 1.9 fusion.9
  (60 shorter events, 13.4 us)
Async XLA Ops:
  8.0 184.2 %reduce-scatter.5.cloned.1.call-start = ((), (), s32[]{:S(2)}) async-start(), calls=%async_computation.4 | async-start | bytes 589824 | tf_op jit(solution)/shard_map/reduce_scatter | solution.py:652
  79.1 1.7 copy-start.1
  115.1 1.6 copy-start
  116.7 8.4 %copy-start.8 = (bf16[1024,1024]{1,0:T(8,128)(2,1)S(1)}, bf16[1024,1024]{1,0:T(8,128)(2,1)}, u32[]{:S(2)}) copy-start(bf16[1024,1024]{1,0:T(8,128)(2,1)} %get-tuple-element.69) | copy-start | bytes 6291460
  125.1 3.4 %copy-start.10 = (bf16[1024,512]{1,0:T(8,128)(2,1)S(1)}, bf16[1024,512]{1,0:T(8,128)(2,1)}, u32[]{:S(2)}) copy-start(bf16[1024,512]{1,0:T(8,128)(2,1)} %get-tuple-element.72) | copy-start | bytes 3145732
  127.8 1.6 copy-start.3
  127.8 65.9 %all-reduce.6.cloned.1.call-start = ((), (), s32[]{:S(2)}) async-start(), calls=%async_computation.2 | async-start | bytes 4194304 | tf_op jit(solution)/shard_map/psum | solution.py:600
  128.4 144.3 %reduce-scatter.3.cloned.1.call-start = ((), (), s32[]{:S(2)}) async-start(), calls=%async_computation.3 | async-start | bytes 3833856 | tf_op jit(solution)/shard_map/reduce_scatter | solution.py:621
  129.4 1.3 copy-start.4
  129.4 1.9 copy-start.9
  129.4 2.2 copy-start.11
  129.4 2.2 copy-start.12
  136.9 1.0 copy-start.5
  136.9 1.0 copy-start.6
  136.9 1.7 copy-start.7
  136.9 56.8 %copy-start.2 = (bf16[1024,1024]{1,0:T(8,128)(2,1)S(1)}, bf16[1024,1024]{1,0:T(8,128)(2,1)}, u32[]{:S(2)}) copy-start(bf16[1024,1024]{1,0:T(8,128)(2,1)} %tok.3) | copy-start | bytes 6291460
Sparse Core Ops, SparseCore 0:
  127.9 64.2 reduce-scatter.4
  195.8 76.8 reduce-scatter.2
Sparse Core Ops, SparseCore 1:
  130.6 52.7 all-reduce.5
